TPU v7x, 32 devices: a whole 2x2x4 slice. The times are simulated.
32 devices in a mesh: fsdp: 32 (over z, y, x, core).
Axes of the slice: x: 2, y: 2, z: 4, core: 2. Of those that a mesh axis runs over, the one named last changes fastest.
Arguments:
- input_one: bfloat16 [32768, 1024], P('fsdp'), may hold values from -6 to 6
- input_two: bfloat16 [32768, 1024], P('fsdp'), may hold values from -6 to 6
- upstream_one: bfloat16 [32768, 1024], P('fsdp'), may hold values from -6 to 6
- upstream_two: bfloat16 [32768, 1024], P('fsdp'), may hold values from -6 to 6
- lengths: int32 [32], replicated, may hold values from 512 to 1024, as said below
- destination: int32 [32], replicated, may hold values from 0 to 31, each once
- buckets: int32 [32, 32, 1024], P('fsdp'), may hold values from 0 to 31
- w_shared: bfloat16 [1024, 1024], P('fsdp'), may hold values from -3 to 3
- w_value: bfloat16 [1024, 1024], P('fsdp'), may hold values from -0.1875 to 0.1875
- w_output: bfloat16 [1024, 1024], P('fsdp'), may hold values from -1.5 to 1.5
- w_expand: bfloat16 [1024, 4096], P('fsdp'), may hold values from -0.1875 to 0.1875
- w_reduce: bfloat16 [4096, 1024], P('fsdp'), may hold values from -0.125 to 0.125
- gain_attend: float32 [1024], P('fsdp'), may hold values from 0.25 to 1.75
- shift_attend: float32 [1024], P('fsdp'), may hold values from -2.5 to 2.5
- gain_mixing: float32 [1024], P('fsdp'), may hold values from 0.25 to 1.75
- shift_mixing: float32 [1024], P('fsdp'), may hold values from -2.5 to 2.5
- bias_output: float32 [1024], P('fsdp'), may hold values from -2.5 to 2.5
- bias_expand: float32 [4096], P('fsdp'), may hold values from -2.5 to 2.5
- bias_reduce: float32 [1024], P('fsdp'), may hold values from -2.5 to 2.5
Outputs:
- result_one: bfloat16 [32768, 1024], P('fsdp')
- result_two: bfloat16 [32768, 1024], P('fsdp')
- grad_one: bfloat16 [32768, 1024], P('fsdp')
- grad_two: bfloat16 [32768, 1024], P('fsdp')
- grad_shared: float32 [1024, 1024], P('fsdp')
- grad_value: float32 [1024, 1024], P('fsdp')
- grad_output: float32 [1024, 1024], P('fsdp')
- grad_expand: float32 [1024, 4096], P('fsdp')
- grad_reduce: float32 [4096, 1024], P('fsdp')
- grad_gain_attend: float32 [1024], P('fsdp')
- grad_shift_attend: float32 [1024], P('fsdp')
- grad_gain_mixing: float32 [1024], P('fsdp')
- grad_shift_mixing: float32 [1024], P('fsdp')
- grad_bias_output: float32 [1024], P('fsdp')
- grad_bias_expand: float32 [4096], P('fsdp')
- grad_bias_reduce: float32 [1024], P('fsdp')
Inputs may be any that keep to these rules, and one draw needn't show every extreme that they name: `lengths`: the longest sequence has exactly 1024 tokens. `destination`: each device index receives exactly one sequence.
All inputs are finite; a program needn't handle non-finite values.
Results may differ from a plain program's by a relative error of at most 0.035.
Values may be sent and summed in bfloat16 or wider, within the bound.
A program may use at most 384 MiB of HBM per device.

v0:
```python
import functools
import math

import jax
import jax.numpy as jnp
from jax import lax
from jax.experimental import pallas as pl
from jax.experimental.pallas import tpu as pltpu
from jax.sharding import PartitionSpec as P

HEADS = 8
DH = 128
GROUP = 64
ROUNDS = 4
BUCKETS = 32
EPS_NORM = 1e-05
EPS_UNIT = 1e-06
LOG2E = math.log2(math.e)
SELF2 = -100000.0 * LOG2E
NEG = -1e30
SCALE = 1.0 / math.sqrt(DH)
TILE = 512
HALF = TILE // 2
KEYS = 256
MANY = TILE // KEYS
STEP = 128.0
SHIFT = 1.5 * 2.0**30
TAME = 3000.0
PAIR = 4
FREE = 99.0
STRIP = 512
AFTER = (2, 4, 6, 8)
CURVE = math.sqrt(2.0 / math.pi)
MESH = pl.DeviceIdType.MESH

NT = (((1,), (1,)), ((), ()))
NN = (((1,), (0,)), ((), ()))
TN = (((0,), (0,)), ((), ()))
F32 = jnp.float32
BF16 = jnp.bfloat16


def dot(a, b, dims=NN):
    return lax.dot_general(a, b, dims, preferred_element_type=F32)


def layer_norm(values, gain, shift):
    center = values - jnp.mean(values, axis=-1, keepdims=True)
    spread = jnp.mean(center * center, axis=-1, keepdims=True)
    return center * lax.rsqrt(spread + EPS_NORM) * gain + shift


def prepare(q, code_ref, spread, ask_s, key_s, h, at):
    lane = lax.broadcasted_iota(jnp.int32, (TILE, DH), 1)
    target = ((lane // 64) * 32 + lane % 16).astype(F32)
    wide = q.astype(F32)
    square = jnp.sum(wide * wide, axis=1, keepdims=True)
    code = dot(code_ref[:, at], spread, TN)
    here = code == target
    ask_s[h, at, :DH] = q
    ask_s[h, at, DH:] = jnp.where(here, STEP, 0.0).astype(BF16)
    key_s[h, at, :DH] = (wide * (lax.rsqrt(square + EPS_UNIT) * (SCALE * LOG2E))).astype(BF16)
    key_s[h, at, DH:] = jnp.where(here | (code + 1.0 == target), 1.0, 0.0).astype(BF16)
    return jnp.max(square)


def lowest(info_ref, i):
    start, stop = i * TILE, (i + 1) * TILE
    one = (info_ref[0] < stop) & (info_ref[1] > start)
    two = (info_ref[2] < stop) & (info_ref[3] > start)
    begin = jnp.where(one, info_ref[0], jnp.where(two, info_ref[2], stop))
    return lax.div(begin, KEYS)


def tile_rows(i):
    return pl.ds(pl.multiple_of(i * TILE, TILE), TILE)


def halves(i):
    start = i * TILE
    return [((0, pl.multiple_of(start, HALF), pl.multiple_of(start, HALF)), HALF),
            ((HALF, pl.multiple_of(start + HALF, HALF), pl.multiple_of(start, HALF)), TILE)]


def part_of(both):
    count = (both + SHIFT) - SHIFT
    return count, both - count


def apart(left, right):
    return dot(left[:, DH:], right[:, DH:], NT), dot(left[:, :DH], right[:, :DH], NT)


def attend_kernel(low_ref, q_ref, v_ref, code_ref, spread_ref, comb_ref, lse_ref, lone_ref, ask_s, key_s, more_s, acc_s, top_s):
    rows = q_ref.shape[0]
    tiles = rows // TILE
    heads = [slice(h * DH, (h + 1) * DH) for h in range(PAIR)]

    def ready(i, largest):
        def fill():
            most = jnp.float32(0.0)
            at = tile_rows(i)
            for h, cols in enumerate(heads):
                most = jnp.maximum(most, prepare(q_ref[at, cols], code_ref, spread_ref[:, cols], ask_s, key_s, h, at))
                more_s[h, at, :DH] = v_ref[at, cols]
                more_s[h, at, DH:] = jnp.ones((TILE, DH), BF16)
            return most

        return jnp.maximum(largest, lax.cond(lowest(low_ref, i) <= (i + 1) * MANY - 1, fill, lambda: jnp.float32(0.0)))

    largest = lax.fori_loop(0, tiles, ready, jnp.float32(0.0))
    tame = largest * (SCALE * LOG2E) ** 2 < TAME
    ask_at = lax.broadcasted_iota(jnp.int32, (TILE, TILE), 0)
    key_at = lax.broadcasted_iota(jnp.int32, (TILE, TILE), 1)

    def finish(h, cols, at, top):
        total = acc_s[h, :, DH:]
        some = total > 0.0
        safe = jnp.where(some, total, 1.0)
        inverse = jnp.where(some, 1.0 / safe, 0.0)
        comb_ref[at, cols] = (acc_s[h, :, :DH] * inverse).astype(BF16)
        lse_ref[h, :, at] = (jnp.log2(safe) + top).T[:1]

    def rows_of(i, carry):
        at = tile_rows(i)
        low = lowest(low_ref, i)

        @pl.when((low < (i + 1) * MANY) & tame)
        def _():
            for h in range(PAIR):
                acc_s[h] = jnp.zeros((TILE, 2 * DH), F32)

            def step(j, carry):
                keys = pl.ds(pl.multiple_of(j * KEYS, KEYS), KEYS)
                for h in range(PAIR):
                    count, score = part_of(dot(ask_s[h, at, :], key_s[h, keys, :], NT))
                    acc_s[h] += dot((count * jnp.exp2(score)).astype(BF16), more_s[h, keys, :])
                return carry

            lax.fori_loop(low, i * MANY, step, 0)
            for h, cols in enumerate(heads):
                for asks, span in halves(i):
                    here = pl.ds(asks[0], HALF)
                    there = pl.ds(asks[1], HALF)
                    keys = pl.ds(asks[2], span)
                    key_at = lax.broadcasted_iota(jnp.int32, (HALF, span), 1)
                    ask_at = lax.broadcasted_iota(jnp.int32, (HALF, span), 0) + (span - HALF)
                    count, score = part_of(dot(ask_s[h, there, :], key_s[h, keys, :], NT))
                    prob = jnp.where(key_at < ask_at, count * jnp.exp2(score), 0.0).astype(BF16)
                    acc_s[h, here, :] += dot(prob, more_s[h, keys, :])
                    active = jnp.max(jnp.where(key_at == ask_at, count, 0.0), axis=1, keepdims=True) > 0.0
                    lone = jnp.where(active & (acc_s[h, here, DH:] == 0.0), 1.0, 0.0)
                    acc_s[h, here, :DH] += lone * v_ref[there, cols].astype(F32)
                    acc_s[h, here, DH:] += lone
                    lone_ref[h, :, there] = lone.T[:1]
                finish(h, cols, at, 0.0)

        @pl.when((low < (i + 1) * MANY) & jnp.logical_not(tame))
        def _():
            for h, cols in enumerate(heads):
                count, score = apart(ask_s[h, at, :], key_s[h, at, :])
                score = jnp.where(key_at == ask_at, SELF2, score)
                score = jnp.where((key_at <= ask_at) & (count > 0.5), score, NEG)
                top = jnp.max(score, axis=1, keepdims=True)
                prob = count * jnp.exp2(score - top)
                acc_s[h] = dot(prob.astype(BF16), more_s[h, at, :])
                top_s[h] = jnp.broadcast_to(top, (TILE, DH))

                def step(j, carry):
                    keys = pl.ds(pl.multiple_of(j * KEYS, KEYS), KEYS)
                    count, score = apart(ask_s[h, at, :], key_s[h, keys, :])
                    score = jnp.where(count > 0.5, score, NEG)
                    top = top_s[h]
                    newer = jnp.maximum(top, jnp.max(score, axis=1, keepdims=True))
                    fade = jnp.exp2(top - newer)
                    prob = count * jnp.exp2(score - newer[:, :1])
                    acc_s[h] = acc_s[h] * jnp.concatenate([fade, fade], axis=1) + dot(prob.astype(BF16), more_s[h, keys, :])
                    top_s[h] = newer
                    return carry

                lax.fori_loop(low, i * MANY, step, 0)
                total = acc_s[h, :, DH:]
                own = STEP * ROUNDS * jnp.exp2(SELF2 - jnp.maximum(top_s[h], SELF2))
                lone_ref[h, :, at] = jnp.where(total > 0.0, own / jnp.where(total > 0.0, total, 1.0), 0.0).T[:1]
                finish(h, cols, at, top_s[h])

        @pl.when(low >= (i + 1) * MANY)
        def _():
            comb_ref[at, :] = jnp.zeros((TILE, PAIR * DH), BF16)
            for h in range(PAIR):
                lse_ref[h, :, at] = jnp.zeros((1, TILE), F32)
                lone_ref[h, :, at] = jnp.zeros((1, TILE), F32)

        return carry

    lax.fori_loop(0, tiles, rows_of, 0)


def back_kernel(
    low_ref, q_ref, v_ref, code_ref, spread_ref, comb_ref, above_ref, lse_ref, lone_ref, *rest,
):
    count = (len(rest) - 9) // 2
    sources, (dq_ref, dv_ref, *targets) = rest[:count], rest[count : 2 * count + 2]
    ask_s, key_s, dunit_s, dvalue_s, dask_s, pass_s, sem = rest[2 * count + 2 :]
    rows = q_ref.shape[0]
    tail_step = pl.num_programs(0) - 1

    def copy_in(k):
        return pltpu.make_async_copy(sources[k], pass_s.at[k], sem.at[k])

    def copy_out(k):
        return pltpu.make_async_copy(pass_s.at[k], targets[k], sem.at[count + k])

    @pl.when(pl.program_id(0) == 0)
    def _():
        for k in range(count):
            copy_in(k).start()

    @pl.when(pl.program_id(0) == tail_step)
    def _():
        for k in range(count):
            copy_in(k).wait()
            copy_out(k).start()

    tiles = rows // TILE
    heads = [slice(h * DH, (h + 1) * DH) for h in range(PAIR)]

    def ready(i, largest):
        def fill():
            most = jnp.float32(0.0)
            at = tile_rows(i)
            for h, cols in enumerate(heads):
                most = jnp.maximum(most, prepare(q_ref[at, cols], code_ref, spread_ref[:, cols], ask_s, key_s, h, at))
                for total in (dunit_s, dvalue_s, dask_s):
                    total[h, at, :] = jnp.zeros((TILE, DH), F32)
            return most

        return jnp.maximum(largest, lax.cond(lowest(low_ref, i) <= (i + 1) * MANY - 1, fill, lambda: jnp.float32(0.0)))

    largest = lax.fori_loop(0, tiles, ready, jnp.float32(0.0))
    tame = largest * (SCALE * LOG2E) ** 2 < TAME

    def pass_over(i, low, split):
        at = tile_rows(i)
        deltas = []
        for h, cols in enumerate(heads):
            mixed = above_ref[at, cols].astype(F32) * comb_ref[at, cols].astype(F32)
            deltas.append(jnp.sum(mixed.T, axis=0, keepdims=True))

        def step(j, carry):
            keys = pl.ds(pl.multiple_of(j * KEYS, KEYS), KEYS)
            for h, cols in enumerate(heads):
                q, above, unit = q_ref[at, cols], above_ref[at, cols], key_s[h, keys, :DH]
                count, score = split(key_s[h, keys, :], ask_s[h, at, :])
                d_prob = dot(v_ref[keys, cols], above, NT)
                prob = count * jnp.exp2(score - lse_ref[h, :, at])
                d_score = (prob * (d_prob - carry[h])).astype(BF16)
                dvalue_s[h, keys, :] += dot(prob.astype(BF16), above)
                dunit_s[h, keys, :] += dot(d_score, q)
                dask_s[h, at, :] += dot(d_score, unit, TN)
            return carry

        deltas = lax.fori_loop(low, i * MANY, step, tuple(deltas))
        for h, cols in enumerate(heads):
            for asks, span in halves(i):
                there = pl.ds(asks[1], HALF)
                keys = pl.ds(asks[2], span)
                key_at = lax.broadcasted_iota(jnp.int32, (span, HALF), 0)
                ask_at = lax.broadcasted_iota(jnp.int32, (span, HALF), 1) + (span - HALF)
                q, above, unit = q_ref[there, cols], above_ref[there, cols], key_s[h, keys, :DH]
                count, score = split(key_s[h, keys, :], ask_s[h, there, :])
                d_prob = dot(v_ref[keys, cols], above, NT)
                prob = count * jnp.exp2(score - lse_ref[h, :, there])
                prob = jnp.where(key_at < ask_at, prob, 0.0)
                d_score = (prob * (d_prob - deltas[h][:, asks[0] : asks[0] + HALF])).astype(BF16)
                prob = jnp.where(key_at == ask_at, lone_ref[h, :, there], prob).astype(BF16)
                dvalue_s[h, keys, :] += dot(prob, above)
                dunit_s[h, keys, :] += dot(d_score, q)
                dask_s[h, there, :] += dot(d_score, unit, TN)

    def together(left, right):
        return part_of(dot(left, right, NT))

    def guarded(left, right):
        count, score = apart(left, right)
        return count, jnp.where(count > 0.5, score, NEG)

    def rows_of(i, carry):
        low = lowest(low_ref, i)

        @pl.when((low < (i + 1) * MANY) & tame)
        def _():
            pass_over(i, low, together)

        @pl.when((low < (i + 1) * MANY) & jnp.logical_not(tame))
        def _():
            pass_over(i, low, guarded)

        return carry

    lax.fori_loop(0, tiles, rows_of, 0)

    def close(i, carry):
        at = tile_rows(i)

        @pl.when(lowest(low_ref, i) <= (i + 1) * MANY - 1)
        def _():
            for h, cols in enumerate(heads):
                q = q_ref[at, cols].astype(F32)
                norm = lax.rsqrt(jnp.sum(q * q, axis=1, keepdims=True) + EPS_UNIT)
                d_unit = dunit_s[h, at, :] * SCALE
                along = jnp.sum(q * d_unit, axis=1, keepdims=True)
                d_q = dask_s[h, at, :] * (1.0 / LOG2E) + d_unit * norm - q * (norm * norm * norm * along)
                dq_ref[at, cols] = d_q.astype(BF16)
                dv_ref[at, cols] = dvalue_s[h, at, :].astype(BF16)

        @pl.when(lowest(low_ref, i) > (i + 1) * MANY - 1)
        def _():
            dq_ref[at, :] = jnp.zeros((TILE, PAIR * DH), BF16)
            dv_ref[at, :] = jnp.zeros((TILE, PAIR * DH), BF16)

        return carry

    lax.fori_loop(0, tiles, close, 0)

    @pl.when(pl.program_id(0) == tail_step)
    def _():
        for k in range(count):
            copy_out(k).wait()


def head_specs(rows):
    by_head = pl.BlockSpec((rows, PAIR * DH), lambda h, low: (0, h))
    code = pl.BlockSpec((ROUNDS * HEADS, rows), lambda h, low: (0, 0))
    spread = pl.BlockSpec((ROUNDS * HEADS, PAIR * DH), lambda h, low: (0, h))
    stat = pl.BlockSpec((PAIR, 1, rows), lambda h, low: (h, 0, 0))
    return by_head, code, spread, stat


def attend(low, shared, values, code, spread):
    rows = shared.shape[0]
    by_head, code_spec, spread_spec, stat = head_specs(rows)
    wide = jax.ShapeDtypeStruct((rows, HEADS * DH), BF16)
    thin = jax.ShapeDtypeStruct((HEADS, 1, rows), F32)
    return pl.pallas_call(
        attend_kernel,
        grid_spec=pltpu.PrefetchScalarGridSpec(
            num_scalar_prefetch=1,
            grid=(HEADS // PAIR,),
            in_specs=[by_head, by_head, code_spec, spread_spec],
            out_specs=[by_head, stat, stat],
            scratch_shapes=[pltpu.VMEM((PAIR, rows, 2 * DH), BF16)] * 3
            + [pltpu.VMEM((PAIR, TILE, 2 * DH), F32), pltpu.VMEM((PAIR, TILE, DH), F32)],
        ),
        out_shape=(wide, thin, thin),
        compiler_params=pltpu.CompilerParams(vmem_limit_bytes=57 << 20),
        name="attend",
        cost_estimate=pl.CostEstimate(
            flops=HEADS * 20 * 3 * 2 * TILE * TILE * DH, bytes_accessed=rows * HEADS * DH * 6, transcendentals=HEADS * 20 * TILE * TILE
        ),
    )(low, shared, values, code, spread)


def attend_back(low, shared, values, code, spread, combined, above, lse, lone, sources):
    rows = shared.shape[0]
    by_head, code_spec, spread_spec, stat = head_specs(rows)
    wide = jax.ShapeDtypeStruct((rows, HEADS * DH), BF16)
    return pl.pallas_call(
        back_kernel,
        grid_spec=pltpu.PrefetchScalarGridSpec(
            num_scalar_prefetch=1,
            grid=(HEADS // PAIR,),
            in_specs=[by_head, by_head, code_spec, spread_spec, by_head, by_head, stat, stat]
            + [pl.BlockSpec(memory_space=pl.ANY)] * len(sources),
            out_specs=[by_head, by_head] + [pl.BlockSpec(memory_space=pl.ANY)] * len(sources),
            scratch_shapes=[pltpu.VMEM((PAIR, rows, 2 * DH), BF16)] * 2 + [pltpu.VMEM((PAIR, rows, DH), F32)] * 3
            + [pltpu.VMEM((len(sources),) + sources[0].shape, BF16), pltpu.SemaphoreType.DMA((2 * len(sources),))],
        ),
        out_shape=(wide, wide) + tuple(jax.ShapeDtypeStruct(source.shape, BF16) for source in sources),
        compiler_params=pltpu.CompilerParams(vmem_limit_bytes=57 << 20),
        name="attend_back",
        cost_estimate=pl.CostEstimate(
            flops=HEADS * 20 * 6 * 2 * TILE * TILE * DH, bytes_accessed=rows * HEADS * DH * 12, transcendentals=HEADS * 20 * TILE * TILE
        ),
    )(low, shared, values, code, spread, combined, above, lse, lone, *sources)


def digits(devices):
    side = 2
    while 8 * side * side < devices:
        side += 1
    assert 8 * side * side == devices, devices
    return 4, side, 2


def neighbours(devices):
    outer, side, core = digits(devices)
    me = lax.axis_index("fsdp")
    c = lax.rem(me, core)
    q = lax.rem(lax.div(me, core), side)
    p = lax.rem(lax.div(me, core * side), side)
    o = lax.div(me, core * side * side)

    def at(o_, p_, q_, c_):
        return ((o_ * side + p_) * side + q_) * core + c_

    core_peer = at(o, p, q, 1 - c)
    q_peers = [(k, at(o, p, k, c)) for k in (lax.rem(q + d, side) for d in range(1, side))]
    p_peers = [(k, at(o, k, q, c)) for k in (lax.rem(p + d, side) for d in range(1, side))]
    o_peers = [(k, at(k, p, q, c)) for k in (lax.rem(o + d, outer) for d in range(1, outer))]
    return (o, p, q, c), core_peer, q_peers, p_peers, o_peers


def peers_of(where):
    return [where[1]] + [device for group in where[2:] for _, device in group]


def greet(peers):
    barrier = pltpu.get_barrier_semaphore()
    for peer in peers:
        pl.semaphore_signal(barrier, inc=1, device_id=(peer,), device_id_type=MESH)
    pl.semaphore_wait(barrier, len(peers))


def remote(src, dst, sems, slot, device):
    return pltpu.make_async_remote_copy(
        src_ref=src, dst_ref=dst, send_sem=sems.at[(0,) + slot], recv_sem=sems.at[(1,) + slot],
        device_id=(device,), device_id_type=MESH,
    )


class Scatter:
    def __init__(self, devices, where, slot, boxes, sems, other, mine, load=None):
        self.outer, self.side, _ = digits(devices)
        (self.o, self.p, self.q, self.c), self.core_peer, self.q_peers, self.p_peers, self.o_peers = where
        self.slot = slot
        self.box_c, box_a0, box_a1, self.box_b, self.box_o = boxes
        self.box_a = (box_a0, box_a1)
        self.sem_c, self.sem_a, self.sem_b, self.sem_o = sems
        self.other, self.mine, self.load = other, mine, load
        half = self.box_o.shape[-1] // 2
        self.columns = (pl.ds(0, half), pl.ds(half, half))

    def core(self):
        return remote(self.other(), self.box_c, self.sem_c, (self.slot,), self.core_peer)

    def first(self, h, d):
        k, device = (self.q_peers, self.p_peers)[h][d]
        spot = (slice(None), slice(None), k) if h == 0 else (slice(None), k, slice(None))
        return remote(self.mine(spot, self.columns[h]), self.box_a[h].at[d], self.sem_a, (self.slot, h, d), device)

    def second(self, h, d):
        k, device = (self.p_peers, self.q_peers)[h][d]
        return remote(
            self.box_a[h].at[0, :, k], self.box_b.at[d, :, :, self.columns[h]], self.sem_b, (self.slot, h, d), device
        )

    def third(self, d):
        k, device = self.o_peers[d]
        return remote(self.box_b.at[0, k], self.box_o.at[d], self.sem_o, (self.slot, d), device)

    def begin(self):
        self.core().start()
        if self.load is not None:
            self.load().start()

    def stage_core(self):
        if self.load is not None:
            self.load().wait()
        self.core().wait_recv()
        side = self.side

        def add(i, carry):
            spot = (lax.div(i, side * side), lax.rem(lax.div(i, side), side), lax.rem(i, side))
            ref = self.mine(spot, slice(None))
            ref[...] = ref[...] + self.box_c[spot]
            return carry

        lax.fori_loop(0, self.outer * side * side, add, 0)
        for h in range(2):
            for d in range(side - 1):
                self.first(h, d).start()

    def stage_first(self):
        side = self.side
        for h in range(2):
            box = self.box_a[h]
            for d in range(side - 1):
                self.first(h, d).wait_recv()

            def add(i, carry):
                a, b = lax.div(i, side), lax.rem(i, side)
                total = self.mine((a, b, self.q) if h == 0 else (a, self.p, b), self.columns[h])[...]
                for d in range(side - 1):
                    total = total + box[d, a, b]
                box[0, a, b] = total
                return carry

            lax.fori_loop(0, self.outer * side, add, 0)
            for d in range(side - 1):
                self.second(h, d).start()

    def stage_second(self):
        box = self.box_b
        for h in range(2):
            k = self.p if h == 0 else self.q
            for d in range(self.side - 1):
                self.second(h, d).wait_recv()

            def add(a, carry):
                total = self.box_a[h][0, a, k]
                for d in range(self.side - 1):
                    total = total + box[d, a, :, self.columns[h]]
                box[0, a, :, self.columns[h]] = total
                return carry

            lax.fori_loop(0, self.outer, add, 0)
        for d in range(self.outer - 1):
            self.third(d).start()

    def stage_third(self):
        total = self.box_b[0, self.o].astype(F32)
        for d in range(self.outer - 1):
            self.third(d).wait_recv()
            total = total + self.box_o[d].astype(F32)
        return total

    def sent_first(self):
        self.core().wait_send()
        for h in range(2):
            for d in range(self.side - 1):
                self.first(h, d).wait_send()

    def sent_last(self):
        for h in range(2):
            for d in range(self.side - 1):
                self.second(h, d).wait_send()
        for d in range(self.outer - 1):
            self.third(d).wait_send()


def boxes_for(devices, rows, width):
    outer, side, _ = digits(devices)
    half = width // 2
    return [
        pltpu.VMEM((outer, side, side, rows, width), BF16),
        pltpu.VMEM((side - 1, outer, side, rows, half), BF16),
        pltpu.VMEM((side - 1, outer, side, rows, half), BF16),
        pltpu.VMEM((side - 1, outer, rows, width), BF16),
        pltpu.VMEM((outer - 1, rows, width), BF16),
    ]


def sems_for(devices, count):
    outer, side, _ = digits(devices)
    dma = pltpu.SemaphoreType.DMA
    return [dma((2, count)), dma((2, count, 2, side - 1)), dma((2, count, 2, side - 1)), dma((2, count, outer - 1))]


def mixing_kernel(
    devices, second_ref, above_ref, expand_ref, reduce_ref, bias_e_ref, bias_r_ref,
    out_ref, back_ref, grad_r_ref, grad_b_ref, grad_e_ref, above_b_ref, act_s, pre_s, grad_s, *rest,
):
    step = pl.program_id(0)
    rows, width = second_ref.shape
    strip = act_s.shape[1]
    per = width // strip
    slices = (len(rest) - 4) // 5
    sems = rest[5 * slices :]
    where = neighbours(devices)
    (o, p, q, c), core_peer, q_peers, p_peers, o_peers = where
    part = grad_s.shape[-2]

    def mover(k):
        def other():
            return grad_s.at[k % 2, :, :, :, 1 - c]

        def mine(spot, cols):
            return grad_s.at[(k % 2,) + tuple(spot) + (c, slice(None), cols)]

        return Scatter(devices, where, k, rest[5 * k : 5 * k + 5], sems, other, mine)

    movers = [mover(k) for k in range(slices)]
    w_e = expand_ref[...].reshape(width, strip)
    w_r = reduce_ref[...].reshape(strip, width)

    @pl.when(step == 0)
    def _():
        greet(peers_of(where))
        out_ref[...] = jnp.broadcast_to(bias_r_ref[...], out_ref.shape)
        back_ref[...] = jnp.zeros(back_ref.shape, F32)
        above_b_ref[...] = jnp.sum(above_ref[...].astype(F32), axis=0, keepdims=True)

    def close(k):
        grad_e_ref[k * part : (k + 1) * part, :] = movers[k].stage_third()

    final = slices * per - 1
    timed, late = [], []
    for k in range(slices):
        begun = 2 * ((k + 1) * per - 1) + 1
        for after, action in zip(
            AFTER, (movers[k].stage_core, movers[k].stage_first, movers[k].stage_second, functools.partial(close, k))
        ):
            if begun + after > 2 * final + 1:
                late.append((begun + after, -k, action))
            else:
                timed.append((begun + after, action))

    def stages(point):
        for when, action in timed:
            if when % 2 == point:
                pl.when(step == when // 2)(action)

    pre = dot(second_ref[...], w_e) + bias_e_ref[...]
    square = pre * pre
    curve = jnp.tanh(CURVE * pre * (1.0 + 0.044715 * square))
    hinge = 0.5 * (1.0 + curve)
    act_s[...] = (pre * hinge).astype(BF16)
    slope = hinge + 0.5 * pre * (1.0 - curve * curve) * (CURVE * (1.0 + 3 * 0.044715 * square))
    d_pre = (dot(above_ref[...], w_r, NT) * slope).astype(BF16)
    pre_s[...] = d_pre
    grad_b_ref[...] = jnp.sum(d_pre.astype(F32), axis=0, keepdims=True)
    stages(0)
    out_ref[...] += dot(act_s[...], w_r)
    back_ref[...] += dot(d_pre, w_e, NT)
    grad_r_ref[...] = dot(act_s[...], above_ref[...], TN).astype(BF16).reshape(grad_r_ref.shape)
    grad_e = dot(second_ref[...], pre_s[...], TN).astype(BF16)
    for k in range(slices):
        for j in range(per):
            @pl.when(step == k * per + j)
            def _():
                if j == 0 and k >= 2:
                    movers[k - 2].sent_first()
                grad_s[k % 2, :, :, :, :, :, j * strip : (j + 1) * strip] = grad_e.reshape(grad_s.shape[1:-1] + (strip,))
                if j == per - 1:
                    movers[k].begin()

    stages(1)

    @pl.when(step == final)
    def _():
        for *_, action in sorted(late, key=lambda entry: entry[:2]):
            action()
        for k in range(max(0, slices - 2), slices):
            movers[k].sent_first()
        for k in range(slices):
            movers[k].sent_last()


def mixing(devices, second, above, gathered, bias_e, bias_r, part):
    rows, width = second.shape
    hidden = bias_e.shape[1]
    many = hidden // devices
    sides = hidden // width
    strip = STRIP
    per = width // strip
    outer, side, core = digits(devices)
    fixed = pl.BlockSpec((rows, width), lambda i: (0, 0), pipeline_mode=pl.Buffered(1))
    whole = pl.BlockSpec(memory_space=pltpu.VMEM)
    scratch = [pltpu.VMEM((rows, strip), BF16)] * 2 + [pltpu.VMEM((2, outer, side, side, core, part, width), BF16)]
    for k in range(sides):
        scratch += boxes_for(devices, part, width)
    return pl.pallas_call(
        functools.partial(mixing_kernel, devices),
        grid=(hidden // strip,),
        in_specs=[
            fixed, fixed,
            pl.BlockSpec((devices, part, strip), lambda i: (0, many // part + 1 + i // per, i % per)),
            pl.BlockSpec((strip // many, many, width), lambda i: (i, 0, 0)),
            pl.BlockSpec((1, strip), lambda i: (0, i)),
            pl.BlockSpec((1, width), lambda i: (0, 0)),
        ],
        out_specs=[
            fixed,
            fixed,
            pl.BlockSpec((strip // many, many, width), lambda i: (i, 0, 0)),
            pl.BlockSpec((1, strip), lambda i: (0, i)),
            pl.BlockSpec((sides * part, width), lambda i: (0, 0)),
            pl.BlockSpec((1, width), lambda i: (0, 0)),
        ],
        out_shape=[
            jax.ShapeDtypeStruct((rows, width), F32),
            jax.ShapeDtypeStruct((rows, width), F32),
            jax.ShapeDtypeStruct((devices, many, width), BF16),
            jax.ShapeDtypeStruct((1, hidden), F32),
            jax.ShapeDtypeStruct((sides * part, width), F32),
            jax.ShapeDtypeStruct((1, width), F32),
        ],
        scratch_shapes=scratch + sems_for(devices, sides),
        compiler_params=pltpu.CompilerParams(collective_id=3, has_side_effects=True, vmem_limit_bytes=57 << 20),
        name="mixing",
    )(second, above, gathered, gathered, bias_e, bias_r)


def join_kernel(
    devices, window_ref, first_ref, final_ref, one_ref, above_ref, live_ref, w_ref, bias_ref, gain_ref, shift_ref,
    combined_ref, out_ref, second_ref, reduce_ref, side_in, part_s, halo_sem,
):
    slots, width = one_ref.shape
    half = slots // 2
    tile = 256
    me = lax.axis_index("fsdp")
    last = devices - 1
    left, right = lax.rem(me + last, devices), lax.rem(me + 1, devices)
    greet([left, right])

    def to_left():
        return remote(window_ref.at[:half], side_in.at[1], halo_sem, (0,), left)

    def to_right():
        return remote(window_ref.at[half + slots :], side_in.at[0], halo_sem, (1,), right)

    @pl.when(me > 0)
    def _():
        to_left().start()

    @pl.when(me < last)
    def _():
        to_right().start()

    @pl.when(me == 0)
    def _():
        side_in[0] = jnp.zeros((half, width), BF16)

    @pl.when(me == last)
    def _():
        side_in[1] = jnp.zeros((half, width), BF16)

    w_o = w_ref[...].reshape(width, width)

    owns = (first_ref, final_ref)

    def before(side, i, carry):
        here = pl.ds(pl.multiple_of(i * tile, tile), tile)
        at = pl.ds(pl.multiple_of(side * half + i * tile, tile), tile)
        part_s[at, :] = dot(owns[side][here, :], w_o)
        reduce_ref[at, :] = (live_ref[at, :] * above_ref[at, :].astype(F32)).astype(BF16)
        return carry

    for side in range(2):
        lax.fori_loop(0, half // tile, functools.partial(before, side), 0)

    def after(side, i, carry):
        here = pl.ds(pl.multiple_of(i * tile, tile), tile)
        at = pl.ds(pl.multiple_of(side * half + i * tile, tile), tile)
        other = side_in[side, here, :]
        combined_ref[at, :] = owns[side][here, :] + other
        attended = part_s[at, :] + dot(other, w_o) + bias_ref[...]
        out = one_ref[at, :].astype(F32) + live_ref[at, :] * attended
        out_ref[at, :] = out
        second_ref[at, :] = layer_norm(out, gain_ref[...], shift_ref[...]).astype(BF16)
        return carry

    @pl.when(me > 0)
    def _():
        to_right().wait_recv()

    lax.fori_loop(0, half // tile, functools.partial(after, 0), 0)

    @pl.when(me < last)
    def _():
        to_left().wait_recv()

    lax.fori_loop(0, half // tile, functools.partial(after, 1), 0)

    @pl.when(me > 0)
    def _():
        to_left().wait_send()

    @pl.when(me < last)
    def _():
        to_right().wait_send()


def join(devices, window, one, above, live, gathered, bias, gain, shift, part, sides):
    slots, width = one.shape
    dma = pltpu.SemaphoreType.DMA
    rows = pl.BlockSpec((slots, width), lambda i: (0, 0))
    thin = pl.BlockSpec((1, width), lambda i: (0, 0))
    low = jax.ShapeDtypeStruct((slots, width), BF16)
    return pl.pallas_call(
        functools.partial(join_kernel, devices),
        grid=(1,),
        in_specs=[
            pl.BlockSpec(memory_space=pl.ANY),
            pl.BlockSpec((slots // 2, width), lambda i: (1, 0)), pl.BlockSpec((slots // 2, width), lambda i: (2, 0)), rows, rows, pl.BlockSpec((slots, 1), lambda i: (0, 0)),
            pl.BlockSpec((devices, part, width), lambda i: (0, sides, 0)), thin, thin, thin,
        ],
        out_specs=[rows] * 4,
        out_shape=[low, jax.ShapeDtypeStruct((slots, width), F32), low, low],
        scratch_shapes=[pltpu.VMEM((2, slots // 2, width), BF16), pltpu.VMEM((slots, width), F32), dma((2, 2))],
        compiler_params=pltpu.CompilerParams(collective_id=6, has_side_effects=True, vmem_limit_bytes=57 << 20),
        name="join",
    )(window, window, window, one, above, live, gathered, bias, gain, shift)


def turn_kernel(
    devices, out_one_ref, d_second_ref, mixed_ref, two_ref, above_ref, combined_ref, live_ref, gain_ref, w_o_ref,
    bias_r_ref, bias_e_ref,
    wide_ref, grad_one_out, one_out, res_two_out, grad_o_out, small_ref,
    mixed_s, two_s, combined_s, one_s, res_two_s, grad_o_s, attend_s, halo_sem, load_sem, store_sem,
):
    slots, width = two_ref.shape
    half = slots // 2
    tile = 256
    part = grad_o_out.shape[1]
    w_o = w_o_ref[...].reshape(width, width)
    me = lax.axis_index("fsdp")
    last = devices - 1
    left, right = lax.rem(me + last, devices), lax.rem(me + 1, devices)
    loads = [
        pltpu.make_async_copy(source, target, load_sem.at[k])
        for k, (source, target) in enumerate(((mixed_ref, mixed_s), (two_ref, two_s), (combined_ref, combined_s)))
    ]
    stores = [
        pltpu.make_async_copy(source, target, store_sem.at[k])
        for k, (source, target) in enumerate(
            ((attend_s, grad_one_out), (one_s, one_out), (res_two_s, res_two_out), (grad_o_s, grad_o_out))
        )
    ]
    for load in loads:
        load.start()
    greet([left, right])

    def to_left():
        return remote(wide_ref.at[half : 2 * half], wide_ref.at[half + slots :], halo_sem, (0,), left)

    def to_right():
        return remote(wide_ref.at[2 * half : 3 * half], wide_ref.at[:half], halo_sem, (1,), right)

    small_ref[...] = jnp.zeros(small_ref.shape, F32)
    gain = gain_ref[...]

    def norm_tile(i, carry):
        at = pl.ds(pl.multiple_of(i * tile, tile), tile)
        live = live_ref[at, :]
        values = out_one_ref[at, :]
        above = d_second_ref[at, :]
        center = values - jnp.mean(values, axis=1, keepdims=True)
        scale = lax.rsqrt(jnp.mean(center * center, axis=1, keepdims=True) + EPS_NORM)
        center = center * scale
        small_ref[2:3, :] += jnp.sum(above * center, axis=0, keepdims=True)
        small_ref[3:4, :] += jnp.sum(above, axis=0, keepdims=True)
        above = above * gain
        mean = jnp.mean(above, axis=1, keepdims=True)
        along = jnp.mean(above * center, axis=1, keepdims=True)
        total = live * (above_ref[at, :].astype(F32) + scale * (above - mean - center * along))
        low = total.astype(BF16)
        attend_s[at, :] = low
        small_ref[4:5, :] += jnp.sum(low.astype(F32), axis=0, keepdims=True)
        wide_ref[pl.ds(pl.multiple_of(half + i * tile, tile), tile), :] = dot(low, w_o, NT).astype(BF16)
        return carry

    lax.fori_loop(0, half // tile, norm_tile, 0)

    @pl.when(me > 0)
    def _():
        to_left().start()

    lax.fori_loop(half // tile, slots // tile, norm_tile, 0)

    @pl.when(me < last)
    def _():
        to_right().start()

    stores[0].start()
    for load in loads:
        load.wait()

    def finish_tile(i, carry):
        at = pl.ds(pl.multiple_of(i * tile, tile), tile)
        live = live_ref[at, :]
        one_s[at, :] = (live * out_one_ref[at, :]).astype(BF16)
        res_two_s[at, :] = (live * (two_s[at, :].astype(F32) + mixed_s[at, :])).astype(BF16)
        return carry

    lax.fori_loop(0, slots // tile, finish_tile, 0)
    stores[1].start()
    stores[2].start()

    def weights(i, carry):
        cols = pl.ds(pl.multiple_of(i * tile, tile), tile)
        many = tile // part
        grad_o_s[pl.ds(pl.multiple_of(i * many, many), many)] = (
            dot(combined_s[:, cols], attend_s[...], TN).astype(BF16).reshape(many, part, width)
        )
        return carry

    lax.fori_loop(0, width // tile, weights, 0)
    stores[3].start()
    small_ref[5:6, :] = bias_r_ref[...]
    for k in range(bias_e_ref.shape[1] // width):
        small_ref[6 + k : 7 + k, :] = bias_e_ref[:, k * width : (k + 1) * width]

    @pl.when(me > 0)
    def _():
        to_right().wait_recv()
        to_left().wait_send()

    @pl.when(me == 0)
    def _():
        wide_ref[:half] = jnp.zeros((half, width), BF16)

    @pl.when(me < last)
    def _():
        to_left().wait_recv()
        to_right().wait_send()

    @pl.when(me == last)
    def _():
        wide_ref[half + slots :] = jnp.zeros((half, width), BF16)

    for store in stores:
        store.wait()


def turn(devices, out_one, d_second, mixed, two, above, combined, live, gain, gathered, bias_r, bias_e, sides):
    slots, width = two.shape
    part = width // devices
    vmem = pl.BlockSpec(memory_space=pltpu.VMEM)
    anywhere = pl.BlockSpec(memory_space=pl.ANY)
    dma = pltpu.SemaphoreType.DMA
    low = pltpu.VMEM((slots, width), BF16)
    rows_low = jax.ShapeDtypeStruct((slots, width), BF16)
    return pl.pallas_call(
        functools.partial(turn_kernel, devices),
        grid=(1,),
        in_specs=[vmem, vmem, anywhere, anywhere, vmem, anywhere, vmem, vmem]
        + [pl.BlockSpec((devices, part, width), lambda i: (0, sides, 0)), vmem, vmem],
        out_specs=(vmem,) + (anywhere,) * 4 + (vmem,),
        out_shape=(
            jax.ShapeDtypeStruct((2 * slots, width), BF16), rows_low, rows_low, rows_low,
            jax.ShapeDtypeStruct((devices, part, width), BF16),
            jax.ShapeDtypeStruct((16, width), F32),
        ),
        scratch_shapes=[
            pltpu.VMEM((slots, width), F32), low, low, low, low, pltpu.VMEM((devices, part, width), BF16), low,
            dma((2, 2)), dma((3,)), dma((4,)),
        ],
        compiler_params=pltpu.CompilerParams(collective_id=5, has_side_effects=True, vmem_limit_bytes=57 << 20),
        name="turn",
    )(out_one, d_second, mixed, two, above, combined, live, gain, gathered, bias_r, bias_e)


def tail_kernel(
    devices, grad_r_ref, grad_o_ref, d_shared_ref, d_value_ref, normed_in, head_ref, own_in, end_ref, above_in, live_ref,
    gain_ref, w_s_ref, w_v_ref, small_ref,
    back_ref, out_s_ref, out_v_ref, out_o_ref, out_r_ref, thin_ref, long_ref,
    normed_ref, own_ref, above_ref, late_sem, side_s, side_in, vector_s, vector_in, grad_s, load_sem, halo_sem, vector_sem, *rest,
):
    window, width = normed_ref.shape
    slots = own_ref.shape[0]
    half = slots // 2
    part = out_s_ref.shape[0]
    many = out_r_ref.shape[0]
    tile = 256
    where = neighbours(devices)
    (o, p, q, c), core_peer, q_peers, p_peers, o_peers = where
    me = lax.axis_index("fsdp")
    outer, side, core = digits(devices)
    owns, rest = rest[:3], rest[3:]
    sems = rest[-4:]

    def distant(source, row, rows, k):
        at = pl.ds(row, rows)

        def other():
            return source.at[:, :, :, 1 - c, at, :]

        def mine(spot, cols):
            return owns[k].at[tuple(spot) + (slice(None), cols)]

        def load():
            return pltpu.make_async_copy(source.at[:, :, :, c, at, :], owns[k], load_sem.at[k])

        return Scatter(devices, where, k, rest[5 * k : 5 * k + 5], sems, other, mine, load)

    def near(j, k):
        def other():
            return grad_s.at[j, :, :, :, 1 - c]

        def mine(spot, cols):
            return grad_s.at[(j,) + tuple(spot) + (c, slice(None), cols)]

        return Scatter(devices, where, k, rest[5 * k : 5 * k + 5], sems, other, mine)

    movers = [
        distant(grad_r_ref, 0, many // 2, 0), distant(grad_r_ref, many // 2, many // 2, 1), distant(grad_o_ref, 0, part, 2),
        near(0, 3), near(1, 4),
    ]
    last = devices - 1
    left, right = lax.rem(me + last, devices), lax.rem(me + 1, devices)
    late = [
        pltpu.make_async_copy(source, target, late_sem.at[k])
        for k, (source, target) in enumerate(((normed_in, normed_ref), (own_in, own_ref), (above_in, above_ref)))
    ]
    for load in late:
        load.start()
    greet(peers_of(where) + [left, right])
    for k in range(3):
        movers[k].begin()

    def to_left():
        return remote(side_s.at[0], side_in.at[1], halo_sem, (0,), left)

    def to_right():
        return remote(side_s.at[1], side_in.at[0], halo_sem, (1,), right)

    vector_s[...] = small_ref[...]
    gain = gain_ref[...]

    def norm_tile(ref, row, at):
        values = ref[pl.ds(row, tile), :].astype(F32)
        above = dot(d_shared_ref[at, :], w_s_ref[...], NT) + dot(d_value_ref[at, :], w_v_ref[...], NT)
        center = values - jnp.mean(values, axis=1, keepdims=True)
        scale = lax.rsqrt(jnp.mean(center * center, axis=1, keepdims=True) + EPS_NORM)
        center = center * scale
        vector_s[0:1, :] += jnp.sum(above * center, axis=0, keepdims=True)
        vector_s[1:2, :] += jnp.sum(above, axis=0, keepdims=True)
        above = above * gain
        mean = jnp.mean(above, axis=1, keepdims=True)
        along = jnp.mean(above * center, axis=1, keepdims=True)
        return scale * (above - mean - center * along)

    def side_tiles(i, carry):
        row = pl.multiple_of(i * tile, tile)
        side_s[0, pl.ds(row, tile), :] = norm_tile(head_ref, row, pl.ds(row, tile)).astype(BF16)
        at = pl.ds(pl.multiple_of(half + slots + i * tile, tile), tile)
        side_s[1, pl.ds(row, tile), :] = norm_tile(end_ref, row, at).astype(BF16)
        return carry

    movers[0].stage_core()
    lax.fori_loop(0, half // tile, side_tiles, 0)

    @pl.when(me > 0)
    def _():
        to_left().start()

    @pl.when(me < last)
    def _():
        to_right().start()

    movers[1].stage_core()
    movers[0].stage_first()

    def weights(j, ref):
        wide = tile // part

        def strip(i, carry):
            cols = pl.ds(pl.multiple_of(i * tile, tile), tile)
            block = dot(normed_ref[:, cols], ref[...], TN).astype(BF16).reshape(wide // core, core, part, width)
            for k in range(wide // core):
                index = i * (wide // core) + k
                spot = (lax.div(index, side * side), lax.rem(lax.div(index, side), side), lax.rem(index, side))
                grad_s[(j,) + spot] = block[k]
            return carry

        lax.fori_loop(0, width // tile, strip, 0)

    for load in late:
        load.wait()
    weights(0, d_shared_ref)
    movers[3].begin()
    movers[2].stage_core()
    movers[1].stage_first()
    movers[0].stage_second()
    weights(1, d_value_ref)
    movers[4].begin()
    movers[3].stage_core()
    movers[2].stage_first()
    movers[1].stage_second()

    def own_tiles(i, carry):
        row = pl.multiple_of(i * tile, tile)
        at = pl.ds(pl.multiple_of(half + i * tile, tile), tile)
        here = pl.ds(row, tile)
        total = above_ref[here, :].astype(F32) + norm_tile(own_ref, row, at)
        back_ref[here, :] = (live_ref[here, :] * total).astype(BF16)
        return carry

    lax.fori_loop(0, slots // tile, own_tiles, 0)

    def vector_copies(stage):
        group = ([(0, core_peer)], q_peers, p_peers, o_peers)[stage]
        base = (0, 1, side, 2 * side - 1)[stage]
        return [
            remote(vector_s if stage == 0 else vector_in.at[base - 1], vector_in.at[base + d], vector_sem, (base + d,), device)
            for d, (_, device) in enumerate(group)
        ]

    def vector_stage(stage):
        base = (0, 1, side, 2 * side - 1)[stage]
        copies = vector_copies(stage)
        total = vector_s[...] if stage == 0 else vector_in[base - 1]
        for d, copy in enumerate(copies):
            copy.wait_recv()
            total = total + vector_in[base + d]
        vector_in[base + len(copies) - 1] = total

    for copy in vector_copies(0):
        copy.start()
    movers[4].stage_core()
    movers[3].stage_first()
    movers[2].stage_second()
    out_r_ref[: many // 2, :] = movers[0].stage_third()
    vector_stage(0)
    for copy in vector_copies(1):
        copy.start()
    movers[4].stage_first()
    movers[3].stage_second()
    out_r_ref[many // 2 :, :] = movers[1].stage_third()
    vector_stage(1)
    for copy in vector_copies(2):
        copy.start()
    movers[4].stage_second()
    out_o_ref[...] = movers[2].stage_third()
    vector_stage(2)
    for copy in vector_copies(3):
        copy.start()

    @pl.when(me > 0)
    def _():
        to_right().wait_recv()

    @pl.when(me == 0)
    def _():
        side_in[0] = jnp.zeros((half, width), BF16)

    @pl.when(me < last)
    def _():
        to_left().wait_recv()

    @pl.when(me == last)
    def _():
        side_in[1] = jnp.zeros((half, width), BF16)

    for k in range(2):
        at = slice(k * half, (k + 1) * half)
        back_ref[at, :] = (back_ref[at, :].astype(F32) + side_in[k].astype(F32)).astype(BF16)
    out_s_ref[...] = movers[3].stage_third()
    vector_stage(3)
    out_v_ref[...] = movers[4].stage_third()
    vectors = 2 * side + outer - 3
    total = vector_in[vectors]
    thin_ref[...] = pltpu.roll(total, lax.rem(width - me * part, width), 1)[:, :DH]
    each = long_ref.shape[1]
    long_rows = [total[6 + k : 7 + k, :] for k in range(devices * each // width)]
    mine = lax.div(me * each, width)
    chosen = long_rows[0]
    for k in range(1, len(long_rows)):
        chosen = jnp.where(mine == k, long_rows[k], chosen)
    long_ref[...] = pltpu.roll(chosen, lax.rem(width - lax.rem(me * each, width), width), 1)[:, :each]
    for stage in range(4):
        for copy in vector_copies(stage):
            copy.wait_send()

    @pl.when(me > 0)
    def _():
        to_left().wait_send()

    @pl.when(me < last)
    def _():
        to_right().wait_send()

    for mover in movers:
        mover.sent_first()
        mover.sent_last()


def tail(devices, grad_r, grad_o, d_shared, d_values, normed, head, own, end, above, live, gain, w_s, w_v, small):
    window, width = normed.shape
    slots = own.shape[0]
    outer, side, core = digits(devices)
    part, many = grad_o.shape[1], grad_r.shape[1]
    each = many
    vmem = pl.BlockSpec(memory_space=pltpu.VMEM)
    anywhere = pl.BlockSpec(memory_space=pl.ANY)
    dma = pltpu.SemaphoreType.DMA
    sizes = [many // 2, many // 2, part, part, part]
    scratch = [
        pltpu.VMEM((window, width), BF16), pltpu.VMEM((slots, width), BF16), pltpu.VMEM((slots, width), BF16), dma((3,)),
        pltpu.VMEM((2, slots // 2, width), BF16), pltpu.VMEM((2, slots // 2, width), BF16),
        pltpu.VMEM((16, width), F32), pltpu.VMEM((2 * side + outer - 2, 16, width), F32),
        pltpu.VMEM((2, outer, side, side, core, part, width), BF16),
        dma((3,)), dma((2, 2)), dma((2, 2 * side + outer - 2)),
    ]
    scratch += [pltpu.VMEM((outer, side, side, rows, width), BF16) for rows in sizes[:3]]
    for rows in sizes:
        scratch += boxes_for(devices, rows, width)
    shape = (outer, side, side, core)
    return pl.pallas_call(
        functools.partial(tail_kernel, devices),
        in_specs=[anywhere, anywhere, vmem, vmem, anywhere, vmem, anywhere, vmem, anywhere] + [vmem] * 5,
        out_specs=(vmem,) * 7,
        out_shape=(
            jax.ShapeDtypeStruct((slots, width), BF16),
            jax.ShapeDtypeStruct((part, width), F32),
            jax.ShapeDtypeStruct((part, width), F32),
            jax.ShapeDtypeStruct((part, width), F32),
            jax.ShapeDtypeStruct((many, width), F32),
            jax.ShapeDtypeStruct((16, DH), F32),
            jax.ShapeDtypeStruct((1, each), F32),
        ),
        scratch_shapes=scratch + sems_for(devices, len(sizes)),
        compiler_params=pltpu.CompilerParams(collective_id=4, has_side_effects=True, vmem_limit_bytes=57 << 20),
        name="tail",
    )(
        grad_r.reshape(shape + grad_r.shape[1:]), grad_o.reshape(shape + grad_o.shape[1:]),
        d_shared, d_values, normed, head, own, end, above, live, gain, w_s, w_v, small,
    )


def find_ranks(length_ref, target_ref, bucket_ref, packed_ref, info_ref, before_s):
    devices = length_ref.shape[0]
    lists, slots = bucket_ref.shape
    me = lax.axis_index("fsdp")
    base = me * slots
    window = 2 * slots

    def look(s, carry):
        start, mine, found, one, two = carry
        size = length_ref[s]
        target = target_ref[s]
        middle = start + lax.shift_right_logical(size, 1)
        inside = (middle >= base) & (middle < base + slots)
        offset = start - base + slots // 2
        entry = (offset, offset + size, target)
        first, second = inside & (found == 0), inside & (found == 1)
        one = tuple(jnp.where(first, new, old) for new, old in zip(entry, one))
        two = tuple(jnp.where(second, new, old) for new, old in zip(entry, two))
        return start + size, jnp.where(target == me, size, mine), found + inside.astype(jnp.int32), one, two

    zero = jnp.int32(0)
    nothing = (jnp.int32(window), jnp.int32(window), zero)
    total, mine, found, one, two = lax.fori_loop(0, devices, look, (zero, zero, zero, nothing, nothing))
    for k, value in enumerate((one[0], one[1], two[0], two[1], one[2], two[2], total, found)):
        info_ref[k] = value

    def fill(i, carry):
        at = pl.ds(pl.multiple_of(i * DH, DH), DH)
        first = lax.broadcasted_iota(jnp.int32, (DH, slots), 0) + i * DH
        second = lax.broadcasted_iota(jnp.int32, (DH, slots), 1)
        before_s[at, :] = jnp.where(first < second, 1.0, 0.0).astype(BF16)
        return carry

    lax.fori_loop(0, slots // DH, fill, 0)
    left = lax.broadcasted_iota(jnp.int32, (DH, DH), 0)
    right = lax.broadcasted_iota(jnp.int32, (DH, DH), 1)
    smaller = jnp.where((left // BUCKETS == right // BUCKETS) & (right < left), 1.0, 0.0).astype(BF16)
    many = DH // BUCKETS
    bucket = lax.broadcasted_iota(jnp.int32, (many, BUCKETS, slots), 1)
    live = lax.broadcasted_iota(jnp.int32, (many, BUCKETS, slots), 2) < mine
    ranks = []
    for g in range(lists // many):
        here = (jnp.broadcast_to(bucket_ref[g * many : (g + 1) * many, :][:, None, :], bucket.shape) == bucket) & live
        one_hot = jnp.where(here, 1.0, 0.0)
        flat = one_hot.reshape(DH, slots).astype(BF16)
        offset = jnp.sum(dot(smaller, flat), axis=1, keepdims=True)
        place = (dot(flat, before_s[...]) + offset).reshape(many, BUCKETS, slots)
        ranks.append(jnp.sum(one_hot * place, axis=1))
    rank = jnp.concatenate(ranks, axis=0)
    live = lax.broadcasted_iota(jnp.int32, (lists, slots), 1) < mine
    packed_ref[:lists, :] = jnp.where(live, jnp.floor(rank * (1.0 / GROUP)), FREE).astype(BF16)


def project_kernel(
    info_ref, head_ref, own_ref, tail_ref, gain_ref, shift_ref, w_s_ref, w_v_ref, one_ref, two_ref,
    normed_ref, shared_ref, value_ref, code_ref,
):
    i = pl.program_id(0)
    tile = own_ref.shape[0]
    steps = pl.num_programs(0)

    def go(ref):
        normed = layer_norm(ref[...].astype(F32), gain_ref[...], shift_ref[...]).astype(BF16)
        normed_ref[...] = normed
        shared_ref[...] = dot(normed, w_s_ref[...]).astype(BF16)
        value_ref[...] = dot(normed, w_v_ref[...]).astype(BF16)

    @pl.when(i < steps // 4)
    def _():
        go(head_ref)

    @pl.when((i >= steps // 4) & (i < steps - steps // 4))
    def _():
        go(own_ref)

    @pl.when(i >= steps - steps // 4)
    def _():
        go(tail_ref)

    @pl.when(i == 0)
    def _():
        lists, window = code_ref.shape
        lane = lax.broadcasted_iota(jnp.int32, (lists, window), 1)
        code = jnp.full((lists, window), FREE, F32)
        for k, ref in enumerate((one_ref, two_ref)):
            begin, end = info_ref[2 * k], info_ref[2 * k + 1]
            rows = ref[0].astype(F32)
            moved = pltpu.roll(jnp.concatenate([rows, rows], axis=1), lax.rem(begin, window), 1)
            code = jnp.where((lane >= begin) & (lane < end), moved + 32.0 * k, code)
        code_ref[...] = code.astype(BF16)


def project(info, head, own, tail, gain, shift, w_s, w_v, blocks):
    slots, width = own.shape
    window = 2 * slots
    lists = ROUNDS * HEADS
    tile = 256
    steps = window // tile
    quarter = steps // 4
    rows = pl.BlockSpec((tile, width), lambda i, info: (i, 0))
    vector = pl.BlockSpec((1, width), lambda i, info: (0, 0))
    matrix = pl.BlockSpec((width, width), lambda i, info: (0, 0), pipeline_mode=pl.Buffered(1))
    wide = jax.ShapeDtypeStruct((window, width), BF16)
    return pl.pallas_call(
        project_kernel,
        grid_spec=pltpu.PrefetchScalarGridSpec(
            num_scalar_prefetch=1,
            grid=(steps,),
            in_specs=[
                pl.BlockSpec((tile, width), lambda i, info: (jnp.minimum(i, quarter - 1), 0)),
                pl.BlockSpec((tile, width), lambda i, info: (jnp.clip(i - quarter, 0, 2 * quarter - 1), 0)),
                pl.BlockSpec((tile, width), lambda i, info: (jnp.clip(i - 3 * quarter, 0, quarter - 1), 0)),
                vector, vector, matrix, matrix,
                pl.BlockSpec((1, lists, slots), lambda i, info: (info[4], 0, 0)),
                pl.BlockSpec((1, lists, slots), lambda i, info: (info[5], 0, 0)),
            ],
            out_specs=[rows, rows, rows, pl.BlockSpec((lists, window), lambda i, info: (0, 0))],
        ),
        out_shape=[wide, wide, wide, jax.ShapeDtypeStruct((lists, window), BF16)],
        compiler_params=pltpu.CompilerParams(vmem_limit_bytes=57 << 20),
        name="project",
    )(info, head, own, tail, gain, shift, w_s, w_v, blocks, blocks)


def gather_kernel(devices, arrays, length_ref, target_ref, bucket_ref, vector_ref, rows_ref, *refs):
    sources, outs, (info_ref, head_ref, end_ref) = refs[: arrays - 1], refs[arrays - 1 : 2 * arrays - 1], refs[2 * arrays - 1 : 2 * arrays + 2]
    packed_s, before_s, own_sem, sem_o, sem_a, sem_b, sem_c, halo_sem, edge_sem = refs[2 * arrays + 2 :]
    sources = sources + (packed_s,)
    outer, side, core = digits(devices)
    (o, p, q, c), core_peer, q_peers, p_peers, o_peers = neighbours(devices)
    me = lax.axis_index("fsdp")
    last_device = devices - 1
    left, right = lax.rem(me + last_device, devices), lax.rem(me + 1, devices)
    greet([core_peer] + [d for _, d in q_peers] + [d for _, d in p_peers] + [d for _, d in o_peers] + [left, right])
    half = sources[0].shape[-1] // 2
    border = head_ref.shape[0]

    def to_left():
        return remote(rows_ref.at[:border], end_ref, halo_sem, (0,), left)

    def to_right():
        return remote(rows_ref.at[border:], head_ref, halo_sem, (1,), right)

    def blank(ref):
        return pltpu.make_async_copy(before_s.at[:border], ref, edge_sem.at[0])

    columns = (pl.ds(0, half), pl.ds(half, half))

    locals_, begun, first, second, last = [], {}, {}, {}, {}
    for s in range(arrays):
        if s == arrays - 1:
            find_ranks(length_ref, target_ref, bucket_ref, packed_s, info_ref, before_s)
            packed_s[bucket_ref.shape[0] :, :] = vector_ref[...]
        locals_.append(pltpu.make_async_copy(sources[s], outs[s].at[o, p, q, c], own_sem.at[s]))
        locals_[s].start()
        for d, (k, device) in enumerate(o_peers):
            begun[s, d] = remote(sources[s], outs[s].at[o, p, q, c], sem_o, (s, d), device)
            begun[s, d].start()

    @pl.when(me > 0)
    def _():
        to_left().start()

    @pl.when(me < last_device)
    def _():
        to_right().start()

    before_s[:border, :] = jnp.zeros((border, before_s.shape[1]), BF16)

    @pl.when(me == 0)
    def _():
        blank(head_ref).start()

    @pl.when(me == last_device)
    def _():
        blank(end_ref).start()

    def stage_a(s):
        locals_[s].wait()
        for d in range(outer - 1):
            begun[s, d].wait_recv()
        for h, peers in enumerate((q_peers, p_peers)):
            piece = outs[s].at[:, p, q, c, :, columns[h]]
            for d, (k, device) in enumerate(peers):
                first[s, h, d] = remote(piece, piece, sem_a, (s, h, d), device)
                first[s, h, d].start()

    def stage_b(s):
        for h, peers in enumerate((p_peers, q_peers)):
            for d in range(side - 1):
                first[s, h, d].wait_recv()
            piece = outs[s].at[:, p, :, c, :, columns[h]] if h == 0 else outs[s].at[:, :, q, c, :, columns[h]]
            for d, (k, device) in enumerate(peers):
                second[s, h, d] = remote(piece, piece, sem_b, (s, h, d), device)
                second[s, h, d].start()

    def stage_c(s):
        for h in range(2):
            for d in range(side - 1):
                second[s, h, d].wait_recv()
        piece = outs[s].at[:, :, :, c]
        last[s] = remote(piece, piece, sem_c, (s,), core_peer)
        last[s].start()

    for t in range(arrays + 2):
        if t < arrays:
            stage_a(t)
        if 0 <= t - 1 < arrays:
            stage_b(t - 1)
        if 0 <= t - 2 < arrays:
            stage_c(t - 2)
    for s in range(arrays):
        last[s].wait_recv()

    @pl.when(me > 0)
    def _():
        to_right().wait_recv()
        to_left().wait_send()

    @pl.when(me == 0)
    def _():
        blank(head_ref).wait()

    @pl.when(me < last_device)
    def _():
        to_left().wait_recv()
        to_right().wait_send()

    @pl.when(me == last_device)
    def _():
        blank(end_ref).wait()

    for group in (begun, first, second, last):
        for copy in group.values():
            copy.wait_send()


def gather(devices, lengths, destination, buckets, vectors, rows, arrays):
    outer, side, core = digits(devices)
    lists, slots = buckets.shape
    packed = jax.ShapeDtypeStruct((lists + vectors.shape[0], slots), BF16)
    shapes = [jax.ShapeDtypeStruct(array.shape, array.dtype) for array in arrays] + [packed]
    count = len(shapes)
    dma = pltpu.SemaphoreType.DMA
    anywhere = pl.BlockSpec(memory_space=pl.ANY)
    hbm = pl.BlockSpec(memory_space=pltpu.HBM)
    smem = pl.BlockSpec(memory_space=pltpu.SMEM)
    vmem = pl.BlockSpec(memory_space=pltpu.VMEM)
    outs = pl.pallas_call(
        functools.partial(gather_kernel, devices, count),
        out_shape=tuple(jax.ShapeDtypeStruct((outer, side, side, core) + shape.shape, shape.dtype) for shape in shapes)
        + (jax.ShapeDtypeStruct((8,), jnp.int32),)
        + (jax.ShapeDtypeStruct((slots // 2, rows.shape[1]), BF16),) * 2,
        in_specs=[smem, smem, vmem, vmem] + [anywhere] * count,
        out_specs=(hbm,) * count + (smem, hbm, hbm),
        scratch_shapes=[
            pltpu.VMEM(packed.shape, BF16), pltpu.VMEM((slots, slots), BF16),
            dma((count,)), dma((2, count, outer - 1)), dma((2, count, 2, side - 1)), dma((2, count, 2, side - 1)), dma((2, count)),
            dma((2, 2)), dma((1,)),
        ],
        compiler_params=pltpu.CompilerParams(collective_id=2, has_side_effects=True, vmem_limit_bytes=57 << 20),
        name="gather",
    )(lengths, destination, buckets, vectors, rows, *arrays)
    return [out.reshape((devices,) + shape.shape) for out, shape in zip(outs, shapes)] + list(outs[count:])


def body(
    input_one, input_two, upstream_one, upstream_two, lengths, destination, buckets,
    w_shared, w_value, w_output, w_expand, w_reduce,
    gain_attend, shift_attend, gain_mixing, shift_mixing, bias_output, bias_expand, bias_reduce,
):
    devices = lax.axis_size("fsdp")
    me = lax.axis_index("fsdp")
    slots, width = input_one.shape
    half = slots // 2
    window = 2 * slots
    part = w_shared.shape[0]
    hidden = w_expand.shape[1]
    sides = hidden // width
    base = me * slots
    lists = ROUNDS * HEADS
    spot = jnp.arange(width, dtype=jnp.int32)
    short = jnp.stack([gain_attend, shift_attend, gain_mixing, shift_mixing, bias_output, bias_reduce])
    short = jnp.where(spot // part == me, jnp.tile(short, (1, devices)), 0.0)
    many = hidden // devices
    long = jnp.tile(bias_expand, width // many)[None]
    long = jnp.where(spot[None] // many + (width // many) * jnp.arange(sides, dtype=jnp.int32)[:, None] == me, long, 0.0)
    vectors = jnp.concatenate([short, long], axis=0)
    high = lax.reduce_precision(vectors, 8, 7)
    count = vectors.shape[0]
    packed = jnp.concatenate(
        [high.astype(BF16), (vectors - high).astype(BF16), jnp.zeros((24 - 2 * count, width), BF16)], axis=0
    )
    second_gather = lax.all_gather(
        jnp.concatenate(
            [w_reduce, w_output] + [w_expand[:, k * width : (k + 1) * width] for k in range(sides)], axis=0
        ),
        "fsdp", axis=0, tiled=False,
    )
    full_shared, full_value, packed, info, two_head, two_tail = gather(
        devices, lengths, destination, buckets[0], packed, input_two, [w_shared, w_value]
    )
    full_shared, full_value = full_shared.reshape(width, width), full_value.reshape(width, width)
    vectors = jnp.sum(packed[:, lists : lists + 2 * count].astype(F32), axis=0)
    vectors = vectors[:count] + vectors[count:]
    gain_a, shift_a, gain_m, shift_m, bias_o, bias_r = (vectors[k : k + 1] for k in range(6))
    bias_e = vectors[6:].reshape(1, hidden)
    lane = jnp.arange(HEADS * DH, dtype=jnp.int32)
    row = jnp.arange(lists, dtype=jnp.int32)[:, None]
    spread = (row == ((lane % 64) // 16) * HEADS + lane // DH).astype(BF16)

    live = ((base + jnp.arange(slots, dtype=jnp.int32)) < info[6]).astype(F32)[:, None]
    normed, shared, values, code = project(
        info, two_head, input_two, two_tail, gain_a, shift_a, full_shared, full_value, packed
    )
    combined_window, lse, lone = attend(info, shared, values, code, spread)
    combined, out_one, second, d_reduce = join(
        devices, combined_window, input_one, upstream_two, live, second_gather, bias_o, gain_m, shift_m, part, sides
    )
    mixed, d_second, grad_reduce, grad_bias_expand, grad_expand, grad_bias_reduce = mixing(
        devices, second, d_reduce, second_gather, bias_e, bias_r, part
    )
    d_combined, grad_one, result_one, result_two, grad_output, small = turn(
        devices, out_one, d_second, mixed, input_two, upstream_one, combined, live, gain_m, second_gather, grad_bias_reduce, grad_bias_expand,
        sides,
    )
    d_shared, d_values, grad_one, result_one, result_two = attend_back(
        info, shared, values, code, spread, combined_window, d_combined, lse, lone, (grad_one, result_one, result_two)
    )
    grad_two, grad_shared, grad_value, grad_output, grad_reduce, thin, long = tail(
        devices, grad_reduce, grad_output, d_shared, d_values, normed,
        two_head, input_two, two_tail, upstream_two, live, gain_a, full_shared, full_value, small,
    )
    return (
        result_one,
        result_two,
        grad_one,
        grad_two,
        grad_shared,
        grad_value,
        grad_output,
        jnp.concatenate([grad_expand[k * part : (k + 1) * part] for k in range(sides)], axis=1),
        grad_reduce,
        thin[0, :part],
        thin[1, :part],
        thin[2, :part],
        thin[3, :part],
        thin[4, :part],
        long.reshape(-1),
        thin[5, :part],
    )


def solution(mesh):
    rows, flat, whole = P("fsdp", None), P("fsdp"), P()
    return jax.shard_map(
        body,
        mesh=mesh,
        in_specs=(rows,) * 4 + (whole, whole, P("fsdp", None, None)) + (rows,) * 5 + (flat,) * 7,
        out_specs=(rows,) * 9 + (flat,) * 7,
        check_vma=False,
    )
```

profile of v0, /device:TPU:0, one launch (start us, length us, event | category | flops | bytes accessed | tf_op | source)
XLA Modules:
  0.0 545.7 jit_solution(17752708994018649407)
XLA Ops:
  7.2 1.0 constant_dynamic-update-slice_fusion.1
  8.2 0.8 constant_dynamic-update-slice_fusion
  9.1 0.8 slice_dynamic-update-slice_fusion.3
  9.9 0.8 slice_dynamic-update-slice_fusion.2
  10.8 0.8 slice_dynamic-update-slice_fusion.1
  11.6 0.8 slice_dynamic-update-slice_fusion
  12.4 0.8 copy-done.3
  13.3 0.8 stack.27
  15.1 92.1 %gather.1 = (bf16[4,2,2,2,32,1024]{5,4,3,2,1,0:T(8,128)(2,1)}, bf16[4,2,2,2,32,1024]{5,4,3,2,1,0:T(8,128)(2,1)}, bf16[4,2,2,2,56,1024]{5,4,3,2,1,0:T(8,128)(2,1)...) custom-call(s32[32]{0:T(128)} %length_ref.1, s32[32]{0:T(128)} %target_ref.1, ...), custom_call_target="tpu_custom_call" | custom-call | tf_op jit(solution)/shard_map/gather/pallas_call | solution.py:1461
  107.2 1.2 slice.80
  108.4 1.7 convert_reduce_fusion
  111.4 18.0 %project.1 = (bf16[2048,1024]{1,0:T(8,128)(2,1)}, bf16[2048,1024]{1,0:T(8,128)(2,1)}, bf16[2048,1024]{1,0:T(8,128)(2,1)}, bf16[32,2048]{1,0:T(8,128)(2,1)}) custom-call(s32[8]{0:T(128)} %get-tuple-element.57.info_ref.low_ref, bf16[512,1024]{1,0:T(8,128)(2,1)} %get-tuple-element.58.head_ref, bf16[1024,1024]{1,0:T(8,128)(2,1)} %own_in.1, ...), custom_call_target="tpu_custom_call" | custom-call | tf_op jit(solution)/shard_map/project/pallas_call | solution.py:1316
  129.4 1.5 fusion.live_ref
  131.5 20.6 %attend.1 = (bf16[2048,1024]{1,0:T(8,128)(2,1)}, f32[8,1,2048]{2,1,0:T(1,128)}, f32[8,1,2048]{2,1,0:T(1,128)}) custom-call(s32[8]{0:T(128)} %get-tuple-element.57.info_ref.low_ref, bf16[2048,1024]{1,0:T(8,128)(2,1)} %get-tuple-element.63.q_ref, bf16[2048,1024]{1,0:T(8,128)(2,1)} %get-tuple-element.64.v_ref, bf16[32,2048]{1,0:T(8,128)(2,1)} %get-tuple-element.65.code_ref, ...), custom_call_target="tpu_custom_call" | custom-call | flops 32212254720 | bytes 12582912 | tf_op jit(solution)/shard_map/attend/pallas_call | solution.py:345
  152.1 22.4 %all-gather.3.cloned.1.call-done = bf16[9216,1024]{1,0:T(8,128)(2,1)} async-done(((bf16[288,1024]{1,0:T(8,128)(2,1)}), bf16[9216,1024]{1,0:T(8,128)(2,1)}) %all-gather.3.cloned.1.call-update) | async-done | bytes 18874384 | tf_op jit(solution)/shard_map/all_gather | solution.py:1506
  174.5 17.7 %join.1 = (bf16[1024,1024]{1,0:T(8,128)(2,1)}, f32[1024,1024]{1,0:T(8,128)}, bf16[1024,1024]{1,0:T(8,128)(2,1)}, bf16[1024,1024]{1,0:T(8,128)(2,1)}) custom-call(bf16[2048,1024]{1,0:T(8,128)(2,1)} %get-tuple-element.66.window_ref.first_ref.final_ref.comb_ref, bf16[2048,1024]{1,0:T(8,128)(2,1)} %get-tuple-element.66.window_ref.first_ref.final_ref.comb_ref, ...), custom_call_target="tpu_custom_call" | custom-call | tf_op jit(solution)/shard_map/join/pallas_call | solution.py:781
  192.2 114.2 %mixing.1 = (f32[1024,1024]{1,0:T(8,128)}, f32[1024,1024]{1,0:T(8,128)}, bf16[32,128,1024]{2,1,0:T(8,128)(2,1)}, f32[1,4096]{1,0:T(1,128)}, f32[128,1024]{1,0:T(8,128)}, /*index=5*/f32[1,1024]{1,0:T(1,128)}) custom-call(bf16[1024,1024]{1,0:T(8,128)(2,1)} %get-tuple-element.68.second_ref, bf16[1024,1024]{1,0:T(8,128)(2,1)} %get-tuple-element.69.above_ref, ...), custom_call_target="tpu_custom_call" | custom-call | tf_op jit(solution)/shard_map/mixing/pallas_call | solution.py:663
  306.5 21.0 %turn.1 = (bf16[2048,1024]{1,0:T(8,128)(2,1)}, bf16[1024,1024]{1,0:T(8,128)(2,1)}, bf16[1024,1024]{1,0:T(8,128)(2,1)}, bf16[1024,1024]{1,0:T(8,128)(2,1)}, bf16[...) custom-call(f32[1024,1024]{1,0:T(8,128)} %get-tuple-element.67.out_one_ref, f32[1024,1024]{1,0:T(8,128)} %get-tuple-element.70.d_second_ref, ...), custom_call_target="tpu_custom_call" | custom-call | tf_op jit(solution)/shard_map/turn/pallas_call | solution.py:925
  327.5 36.2 %attend_back.1 = (bf16[2048,1024]{1,0:T(8,128)(2,1)}, bf16[2048,1024]{1,0:T(8,128)(2,1)}, bf16[1024,1024]{1,0:T(8,128)(2,1)}, bf16[1024,1024]{1,0:T(8,128)(2,1)}, bf16[1024,1024]{1,0:T(8,128)(2,1)}) custom-call(s32[8]{0:T(128)} %get-tuple-element.57.info_ref.low_ref, bf16[2048,1024]{1,0:T(8,128)(2,1)} %get-tuple-element.63.q_ref, ...), custom_call_target="tpu_custom_call" | custom-call | flops 64424509440 | bytes 25165824 | tf_op jit(solution)/shard_map/attend_back/pallas_call | solution.py:368
  363.7 168.0 %tail.1 = (bf16[1024,1024]{1,0:T(8,128)(2,1)}, f32[32,1024]{1,0:T(8,128)}, f32[32,1024]{1,0:T(8,128)}, f32[32,1024]{1,0:T(8,128)}, f32[128,1024]{1,0:T(8,128)}, /*index=5*/f32[16,128]{1,0:T(8,128)}, f32[1,128]{1,0:T(1,128)}) custom-call(bf16[4,2,2,2,128,1024]{5,4,3,2,1,0:T(8,128)(2,1)} %bitcast.40, bf16[4,2,2,2,32,1024]{5,4,3,2,1,0:T(8,128)(2,1)} %bitcast.45, ...), custom_call_target="tpu_custom_call" | custom-call | tf_op jit(solution)/shard_map/tail/pallas_call | solution.py:1191
  531.7 1.4 slice_bitcast_fusion.1
  533.1 0.8 pad_maximum_fusion
  534.0 1.3 copy.47
  537.3 0.8 copy.51
  (44 shorter events, 5.5 us)
Async XLA Ops:
  7.2 7.1 %copy-start = (f32[128]{0:T(128)S(1)}, f32[128]{0:T(128)}, u32[]{:S(2)}) copy-start(f32[128]{0:T(128)} %param.36) | copy-start | bytes 1540
  7.2 167.3 %all-gather.3.cloned.1.call-start = ((), (), s32[]{:S(2)}) async-start(), calls=%async_computation | async-start | bytes 19464192 | tf_op jit(solution)/shard_map/all_gather | solution.py:1506
  12.4 0.8 copy-start.3
  363.7 169.4 %copy-start.4 = (f32[128,1024]{1,0:T(8,128)S(1)}, f32[128,1024]{1,0:T(8,128)}, u32[]{:S(2)}) copy-start(f32[128,1024]{1,0:T(8,128)} %get-tuple-element.94) | copy-start | bytes 1572868
  531.6 2.3 copy-start.2
  534.0 4.7 copy-start.1
  534.0 1.4 copy-start.8
  534.0 2.0 copy-start.7
  534.0 2.7 copy-start.6
  534.0 3.3 copy-start.5
  534.0 4.1 copy-start.9
Sparse Core Ops, SparseCore 0:
  13.4 161.0 all-gather.2
where the time goes:
time: 552 us; the launch traced here: 546 us
  Pallas kernels  488 us (88%)
  waiting for transfers between devices  22.4 us (4%)
  local copies, waits for them, and re-layouts  15.5 us (3%)
  between operations  14.5 us (3%)
  other arithmetic  5.53 us (1%)
    pallas_call x1, Pallas kernels, tail(): pl.pallas_call(functools.partial(tail_kernel, devices), in_specs=[anywher...  168 us
    pallas_call x1, Pallas kernels, mixing(): pl.pallas_call(functools.partial(mixing_kernel, devices), grid=(hidden //...  114 us
    pallas_call x1, Pallas kernels, gather(): pl.pallas_call(functools.partial(gather_kernel, devices, count), out_shap...  92.1 us
    pallas_call x1, Pallas kernels, attend_back(): pl.pallas_call(back_kernel, grid_spec=pltpu.PrefetchScalarGridSpec(num_sc...  36.2 us
    all_gather x1, waiting for transfers between devices, body(): lax.all_gather(jnp.concatenate([w_reduce, w_output] + [w_expand[:, k * wi...  22.4 us
    pallas_call x1, Pallas kernels, turn(): pl.pallas_call(functools.partial(turn_kernel, devices), grid=(1,), in_spe...  21 us
    pallas_call x1, Pallas kernels, attend(): pl.pallas_call(attend_kernel, grid_spec=pltpu.PrefetchScalarGridSpec(num_...  20.6 us
    pallas_call x1, Pallas kernels, project(): pl.pallas_call(project_kernel, grid_spec=pltpu.PrefetchScalarGridSpec(num...  18 us
  transfers between devices with their start and end apart: 1, of which 1 were waited for; matrix products, arithmetic and copies ran while one was open for 1% of the time, Pallas kernels for 24%

commit v1 on v0

--- a/solution.py
+++ b/solution.py
@@ -958,7 +958,7 @@
     (o, p, q, c), core_peer, q_peers, p_peers, o_peers = where
     me = lax.axis_index("fsdp")
     outer, side, core = digits(devices)
-    owns, rest = rest[:3], rest[3:]
+    owns, rest = rest[:5], rest[5:]
     sems = rest[-4:]
 
     def distant(source, row, rows, k):
@@ -984,10 +984,27 @@
 
         return Scatter(devices, where, k, rest[5 * k : 5 * k + 5], sems, other, mine)
 
-    movers = [
-        distant(grad_r_ref, 0, many // 2, 0), distant(grad_r_ref, many // 2, many // 2, 1), distant(grad_o_ref, 0, part, 2),
-        near(0, 3), near(1, 4),
-    ]
+    quarter = many // 4
+    movers = [distant(grad_r_ref, k * quarter, quarter, k) for k in range(4)]
+    movers += [distant(grad_o_ref, 0, part, 4), near(0, 5), near(1, 6)]
+
+    def third(k):
+        total = movers[k].stage_third()
+        if k < 4:
+            out_r_ref[k * quarter : (k + 1) * quarter, :] = total
+        else:
+            (out_o_ref, out_s_ref, out_v_ref)[k - 4][...] = total
+
+    def tick(t):
+        if t < 7:
+            movers[t].stage_core()
+        if 0 <= t - 1 < 7:
+            movers[t - 1].stage_first()
+        if 0 <= t - 2 < 7:
+            movers[t - 2].stage_second()
+        if 0 <= t - 3 < 7:
+            third(t - 3)
+
     last = devices - 1
     left, right = lax.rem(me + last, devices), lax.rem(me + 1, devices)
     late = [
@@ -997,7 +1014,7 @@
     for load in late:
         load.start()
     greet(peers_of(where) + [left, right])
-    for k in range(3):
+    for k in range(5):
         movers[k].begin()
 
     def to_left():
@@ -1029,7 +1046,7 @@
         side_s[1, pl.ds(row, tile), :] = norm_tile(end_ref, row, at).astype(BF16)
         return carry
 
-    movers[0].stage_core()
+    tick(0)
     lax.fori_loop(0, half // tile, side_tiles, 0)
 
     @pl.when(me > 0)
@@ -1040,8 +1057,8 @@
     def _():
         to_right().start()
 
-    movers[1].stage_core()
-    movers[0].stage_first()
+    tick(1)
+    tick(2)
 
     def weights(j, ref):
         wide = tile // part
@@ -1060,15 +1077,12 @@
     for load in late:
         load.wait()
     weights(0, d_shared_ref)
-    movers[3].begin()
-    movers[2].stage_core()
-    movers[1].stage_first()
-    movers[0].stage_second()
+    movers[5].begin()
+    tick(3)
+    tick(4)
     weights(1, d_value_ref)
-    movers[4].begin()
-    movers[3].stage_core()
-    movers[2].stage_first()
-    movers[1].stage_second()
+    movers[6].begin()
+    tick(5)
 
     def own_tiles(i, carry):
         row = pl.multiple_of(i * tile, tile)
@@ -1099,24 +1113,11 @@
 
     for copy in vector_copies(0):
         copy.start()
-    movers[4].stage_core()
-    movers[3].stage_first()
-    movers[2].stage_second()
-    out_r_ref[: many // 2, :] = movers[0].stage_third()
-    vector_stage(0)
-    for copy in vector_copies(1):
-        copy.start()
-    movers[4].stage_first()
-    movers[3].stage_second()
-    out_r_ref[many // 2 :, :] = movers[1].stage_third()
-    vector_stage(1)
-    for copy in vector_copies(2):
-        copy.start()
-    movers[4].stage_second()
-    out_o_ref[...] = movers[2].stage_third()
-    vector_stage(2)
-    for copy in vector_copies(3):
-        copy.start()
+    for stage in range(3):
+        tick(6 + stage)
+        vector_stage(stage)
+        for copy in vector_copies(stage + 1):
+            copy.start()
 
     @pl.when(me > 0)
     def _():
@@ -1137,9 +1138,8 @@
     for k in range(2):
         at = slice(k * half, (k + 1) * half)
         back_ref[at, :] = (back_ref[at, :].astype(F32) + side_in[k].astype(F32)).astype(BF16)
-    out_s_ref[...] = movers[3].stage_third()
     vector_stage(3)
-    out_v_ref[...] = movers[4].stage_third()
+    tick(9)
     vectors = 2 * side + outer - 3
     total = vector_in[vectors]
     thin_ref[...] = pltpu.roll(total, lax.rem(width - me * part, width), 1)[:, :DH]
@@ -1176,15 +1176,15 @@
     vmem = pl.BlockSpec(memory_space=pltpu.VMEM)
     anywhere = pl.BlockSpec(memory_space=pl.ANY)
     dma = pltpu.SemaphoreType.DMA
-    sizes = [many // 2, many // 2, part, part, part]
+    sizes = [many // 4] * 4 + [part] * 3
     scratch = [
         pltpu.VMEM((window, width), BF16), pltpu.VMEM((slots, width), BF16), pltpu.VMEM((slots, width), BF16), dma((3,)),
         pltpu.VMEM((2, slots // 2, width), BF16), pltpu.VMEM((2, slots // 2, width), BF16),
         pltpu.VMEM((16, width), F32), pltpu.VMEM((2 * side + outer - 2, 16, width), F32),
         pltpu.VMEM((2, outer, side, side, core, part, width), BF16),
-        dma((3,)), dma((2, 2)), dma((2, 2 * side + outer - 2)),
+        dma((5,)), dma((2, 2)), dma((2, 2 * side + outer - 2)),
     ]
-    scratch += [pltpu.VMEM((outer, side, side, rows, width), BF16) for rows in sizes[:3]]
+    scratch += [pltpu.VMEM((outer, side, side, rows, width), BF16) for rows in sizes[:5]]
     for rows in sizes:
         scratch += boxes_for(devices, rows, width)
     shape = (outer, side, side, core)
@@ -1306,7 +1306,7 @@
     slots, width = own.shape
     window = 2 * slots
     lists = ROUNDS * HEADS
-    tile = 256
+    tile = 512
     steps = window // tile
     quarter = steps // 4
     rows = pl.BlockSpec((tile, width), lambda i, info: (i, 0))

time: 552 us -> 557 us (level)
    pallas_call x1, Pallas kernels: 17.7 us -> 27.8 us  [join(): pl.pallas_call(functools.partial(join_kernel, devices), grid=(1,), in_spe...]
    pallas_call x1, Pallas kernels: 114 us -> 107 us  [mixing(): pl.pallas_call(functools.partial(mixing_kernel, devices), grid=(hidden //...]
where the time goes in v1:
time: 557 us; the launch traced here: 546 us
  Pallas kernels  488 us (88%)
  waiting for transfers between devices  22.8 us (4%)
  local copies, waits for them, and re-layouts  15.5 us (3%)
  between operations  14.7 us (3%)
    pallas_call x1, Pallas kernels, tail(): pl.pallas_call(functools.partial(tail_kernel, devices), in_specs=[anywher...  166 us
    pallas_call x1, Pallas kernels, mixing(): pl.pallas_call(functools.partial(mixing_kernel, devices), grid=(hidden //...  107 us
    pallas_call x1, Pallas kernels, gather(): pl.pallas_call(functools.partial(gather_kernel, devices, count), out_shap...  92.1 us
    pallas_call x1, Pallas kernels, attend_back(): pl.pallas_call(back_kernel, grid_spec=pltpu.PrefetchScalarGridSpec(num_sc...  36.2 us
    pallas_call x1, Pallas kernels, join(): pl.pallas_call(functools.partial(join_kernel, devices), grid=(1,), in_spe...  27.8 us
    all_gather x1, waiting for transfers between devices, body(): lax.all_gather(jnp.concatenate([w_reduce, w_output] + [w_expand[:, k * wi...  22.8 us
    pallas_call x1, Pallas kernels, turn(): pl.pallas_call(functools.partial(turn_kernel, devices), grid=(1,), in_spe...  21.1 us
    pallas_call x1, Pallas kernels, attend(): pl.pallas_call(attend_kernel, grid_spec=pltpu.PrefetchScalarGridSpec(num_...  20.6 us
  transfers between devices with their start and end apart: 1, of which 1 were waited for; matrix products, arithmetic and copies ran while one was open for 1% of the time, Pallas kernels for 24%

profile of v1, /device:TPU:0, one launch (start us, length us, event | category | flops | bytes accessed | tf_op | source)
XLA Modules:
  0.0 546.2 jit_solution(15652644361677251713)
XLA Ops:
  7.2 1.0 constant_dynamic-update-slice_fusion.1
  8.2 0.8 constant_dynamic-update-slice_fusion
  9.1 0.8 slice_dynamic-update-slice_fusion.3
  9.9 0.8 slice_dynamic-update-slice_fusion.2
  10.8 0.8 slice_dynamic-update-slice_fusion.1
  11.6 0.8 slice_dynamic-update-slice_fusion
  12.4 0.8 copy-done.3
  13.3 0.8 stack.27
  15.1 92.1 %gather.1 = (bf16[4,2,2,2,32,1024]{5,4,3,2,1,0:T(8,128)(2,1)}, bf16[4,2,2,2,32,1024]{5,4,3,2,1,0:T(8,128)(2,1)}, bf16[4,2,2,2,56,1024]{5,4,3,2,1,0:T(8,128)(2,1)...) custom-call(s32[32]{0:T(128)} %length_ref.1, s32[32]{0:T(128)} %target_ref.1, ...), custom_call_target="tpu_custom_call" | custom-call | tf_op jit(solution)/shard_map/gather/pallas_call | solution.py:1461
  107.2 1.2 slice.80
  108.4 1.7 convert_reduce_fusion
  111.4 17.5 %project.1 = (bf16[2048,1024]{1,0:T(8,128)(2,1)}, bf16[2048,1024]{1,0:T(8,128)(2,1)}, bf16[2048,1024]{1,0:T(8,128)(2,1)}, bf16[32,2048]{1,0:T(8,128)(2,1)}) custom-call(s32[8]{0:T(128)} %get-tuple-element.57.info_ref.low_ref, bf16[512,1024]{1,0:T(8,128)(2,1)} %get-tuple-element.58.head_ref, bf16[1024,1024]{1,0:T(8,128)(2,1)} %own_in.1, ...), custom_call_target="tpu_custom_call" | custom-call | tf_op jit(solution)/shard_map/project/pallas_call | solution.py:1316
  128.9 1.5 fusion.live_ref
  131.1 20.6 %attend.1 = (bf16[2048,1024]{1,0:T(8,128)(2,1)}, f32[8,1,2048]{2,1,0:T(1,128)}, f32[8,1,2048]{2,1,0:T(1,128)}) custom-call(s32[8]{0:T(128)} %get-tuple-element.57.info_ref.low_ref, bf16[2048,1024]{1,0:T(8,128)(2,1)} %get-tuple-element.63.q_ref, bf16[2048,1024]{1,0:T(8,128)(2,1)} %get-tuple-element.64.v_ref, bf16[32,2048]{1,0:T(8,128)(2,1)} %get-tuple-element.65.code_ref, ...), custom_call_target="tpu_custom_call" | custom-call | flops 32212254720 | bytes 12582912 | tf_op jit(solution)/shard_map/attend/pallas_call | solution.py:345
  151.7 22.8 %all-gather.3.cloned.1.call-done = bf16[9216,1024]{1,0:T(8,128)(2,1)} async-done(((bf16[288,1024]{1,0:T(8,128)(2,1)}), bf16[9216,1024]{1,0:T(8,128)(2,1)}) %all-gather.3.cloned.1.call-update) | async-done | bytes 18874384 | tf_op jit(solution)/shard_map/all_gather | solution.py:1506
  174.5 27.8 %join.1 = (bf16[1024,1024]{1,0:T(8,128)(2,1)}, f32[1024,1024]{1,0:T(8,128)}, bf16[1024,1024]{1,0:T(8,128)(2,1)}, bf16[1024,1024]{1,0:T(8,128)(2,1)}) custom-call(bf16[2048,1024]{1,0:T(8,128)(2,1)} %get-tuple-element.66.window_ref.first_ref.final_ref.comb_ref, bf16[2048,1024]{1,0:T(8,128)(2,1)} %get-tuple-element.66.window_ref.first_ref.final_ref.comb_ref, ...), custom_call_target="tpu_custom_call" | custom-call | tf_op jit(solution)/shard_map/join/pallas_call | solution.py:781
  202.3 106.6 %mixing.1 = (f32[1024,1024]{1,0:T(8,128)}, f32[1024,1024]{1,0:T(8,128)}, bf16[32,128,1024]{2,1,0:T(8,128)(2,1)}, f32[1,4096]{1,0:T(1,128)}, f32[128,1024]{1,0:T(8,128)}, /*index=5*/f32[1,1024]{1,0:T(1,128)}) custom-call(bf16[1024,1024]{1,0:T(8,128)(2,1)} %get-tuple-element.68.second_ref, bf16[1024,1024]{1,0:T(8,128)(2,1)} %get-tuple-element.69.above_ref, ...), custom_call_target="tpu_custom_call" | custom-call | tf_op jit(solution)/shard_map/mixing/pallas_call | solution.py:663
  308.9 21.1 %turn.1 = (bf16[2048,1024]{1,0:T(8,128)(2,1)}, bf16[1024,1024]{1,0:T(8,128)(2,1)}, bf16[1024,1024]{1,0:T(8,128)(2,1)}, bf16[1024,1024]{1,0:T(8,128)(2,1)}, bf16[...) custom-call(f32[1024,1024]{1,0:T(8,128)} %get-tuple-element.67.out_one_ref, f32[1024,1024]{1,0:T(8,128)} %get-tuple-element.70.d_second_ref, ...), custom_call_target="tpu_custom_call" | custom-call | tf_op jit(solution)/shard_map/turn/pallas_call | solution.py:925
  330.1 36.2 %attend_back.1 = (bf16[2048,1024]{1,0:T(8,128)(2,1)}, bf16[2048,1024]{1,0:T(8,128)(2,1)}, bf16[1024,1024]{1,0:T(8,128)(2,1)}, bf16[1024,1024]{1,0:T(8,128)(2,1)}, bf16[1024,1024]{1,0:T(8,128)(2,1)}) custom-call(s32[8]{0:T(128)} %get-tuple-element.57.info_ref.low_ref, bf16[2048,1024]{1,0:T(8,128)(2,1)} %get-tuple-element.63.q_ref, ...), custom_call_target="tpu_custom_call" | custom-call | flops 64424509440 | bytes 25165824 | tf_op jit(solution)/shard_map/attend_back/pallas_call | solution.py:368
  366.3 165.6 %tail.1 = (bf16[1024,1024]{1,0:T(8,128)(2,1)}, f32[32,1024]{1,0:T(8,128)}, f32[32,1024]{1,0:T(8,128)}, f32[32,1024]{1,0:T(8,128)}, f32[128,1024]{1,0:T(8,128)}, /*index=5*/f32[16,128]{1,0:T(8,128)}, f32[1,128]{1,0:T(1,128)}) custom-call(bf16[4,2,2,2,128,1024]{5,4,3,2,1,0:T(8,128)(2,1)} %bitcast.40, bf16[4,2,2,2,32,1024]{5,4,3,2,1,0:T(8,128)(2,1)} %bitcast.45, ...), custom_call_target="tpu_custom_call" | custom-call | tf_op jit(solution)/shard_map/tail/pallas_call | solution.py:1191
  532.0 1.4 slice_bitcast_fusion.1
  533.4 0.8 pad_maximum_fusion
  534.3 1.3 copy.47
  537.6 0.8 copy.51
  (44 shorter events, 5.5 us)
Async XLA Ops:
  7.2 7.1 %copy-start = (f32[128]{0:T(128)S(1)}, f32[128]{0:T(128)}, u32[]{:S(2)}) copy-start(f32[128]{0:T(128)} %param.36) | copy-start | bytes 1540
  7.2 167.3 %all-gather.3.cloned.1.call-start = ((), (), s32[]{:S(2)}) async-start(), calls=%async_computation | async-start | bytes 19464192 | tf_op jit(solution)/shard_map/all_gather | solution.py:1506
  12.4 0.8 copy-start.3
  366.3 167.1 %copy-start.4 = (f32[128,1024]{1,0:T(8,128)S(1)}, f32[128,1024]{1,0:T(8,128)}, u32[]{:S(2)}) copy-start(f32[128,1024]{1,0:T(8,128)} %get-tuple-element.94) | copy-start | bytes 1572868
  531.9 2.3 copy-start.2
  534.3 4.7 copy-start.1
  534.3 1.4 copy-start.8
  534.3 2.0 copy-start.7
  534.3 2.7 copy-start.6
  534.3 3.3 copy-start.5
  534.3 4.1 copy-start.9
Sparse Core Ops, SparseCore 0:
  13.4 161.0 all-gather.2
